TPU v7x, 1024 devices: a whole 4x8x16 slice. The times are simulated.
1024 devices in a mesh: kx: 32 (over x_hi, y, core), ky: 32 (over x_lo, z).
Axes of the slice: x: 4 (x_hi: 2, x_lo: 2; x = x_hi * 2 + x_lo), y: 8, z: 16, core: 2. Of those that a mesh axis runs over, the one named last changes fastest.
Arguments:
- block: bfloat16 [32, 32, 2, 2, 128, 128], P('kx', 'ky'), may hold values from -4 to 4
- history: bfloat16 [32, 32, 2, 2, 128, 128], P('kx', 'ky'), may hold values from -0.5 to 0.5
Outputs:
- collision: float32 [32, 32, 2, 2, 128, 128], P('kx', 'ky')
All inputs are finite; a program needn't handle non-finite values.
Results may differ from a plain program's by a relative error of at most 0.028.
Values may be sent and summed in bfloat16 or wider, within the bound.
A program may use at most 32 MiB of HBM per device.

v0:
```python
import math

import jax
import jax.numpy as jnp
from jax import lax
from jax.sharding import PartitionSpec as P

ITERS = 2


coupling = 0.5


def shortened(x):

    def short(part):
        return part.astype(jnp.bfloat16) if part.dtype == jnp.float32 else part

    return jax.tree.map(short, x)


def joint_table(extent, sign):
    positions = jnp.arange(extent, dtype=jnp.int32)
    phases = positions[:, None] * positions[None, :] % extent
    angles = phases.astype(jnp.float32) * (2.0 * math.pi / extent)
    factor = 1.0 / math.sqrt(extent)
    cosine = jnp.cos(angles) * factor
    sine_table = jnp.sin(angles) * (sign * factor)
    upper = jnp.concatenate((cosine, -sine_table), 1)
    lower = jnp.concatenate((sine_table, cosine), 1)
    return jnp.concatenate((upper, lower), 0)


def transform(real_part, imag_part, axis, sign):
    extent = real_part.shape[axis]
    table = joint_table(extent, sign)
    stacked = jnp.concatenate((real_part, imag_part), axis)
    letters = "abcdefgh"[: stacked.ndim]
    target = letters[:axis] + "z" + letters[axis + 1 :]
    form = "z" + letters[axis] + "," + letters + "->" + target
    result = jnp.einsum(form, table, stacked, precision=lax.Precision.HIGH)
    new_real = lax.slice_in_dim(result, 0, extent, axis=axis)
    new_imag = lax.slice_in_dim(result, extent, 2 * extent, axis=axis)
    return (new_real, new_imag)


def mirror(field):
    return jnp.roll(jnp.flip(field, (0, 1)), (1, 1), (0, 1))


def complex_times(left_real, left_imag, right_real, right_imag):
    return (
        left_real * right_real - left_imag * right_imag,
        left_real * right_imag + left_imag * right_real,
    )


def self_energy(site_real, site_imag):
    ret_real, ret_imag = (site_real[:, :, 0], site_imag[:, :, 0])
    les_real, les_imag = (site_real[:, :, 1], site_imag[:, :, 1])
    square_real, square_imag = complex_times(ret_real, ret_imag, ret_real, ret_imag)
    self_ret = complex_times(square_real, square_imag, mirror(les_real), -mirror(les_imag))
    square_real, square_imag = complex_times(les_real, les_imag, les_real, les_imag)
    self_les = complex_times(square_real, square_imag, mirror(ret_real), -mirror(ret_imag))
    out_real = jnp.stack((self_ret[0], self_les[0]), 2).astype(jnp.bfloat16)
    out_imag = jnp.stack((self_ret[1], self_les[1]), 2).astype(jnp.bfloat16)
    return (out_real, out_imag)


def to_sites(current):
    along_x = lax.all_to_all(current, "kx", split_axis=4, concat_axis=0, tiled=True).astype(
        jnp.float32
    )
    first_real, first_imag = transform(along_x[:, :, :, 0], along_x[:, :, :, 1], 0, 1.0)
    stacked = jnp.stack((first_real, first_imag), 3)
    along_y = lax.all_to_all(
        shortened(stacked), "ky", split_axis=5, concat_axis=1, tiled=True
    ).astype(stacked.dtype)
    return transform(along_y[:, :, :, 0], along_y[:, :, :, 1], 1, 1.0)


def to_momenta(self_real, self_imag):
    self_real, self_imag = lax.optimization_barrier((self_real, self_imag))
    wide_real = self_real.astype(jnp.float32)
    wide_imag = self_imag.astype(jnp.float32)
    first_real, first_imag = transform(wide_real, wide_imag, 1, -1.0)
    stacked = jnp.stack((first_real, first_imag), 3)
    along_y = lax.all_to_all(
        shortened(stacked), "ky", split_axis=1, concat_axis=5, tiled=True
    ).astype(stacked.dtype)
    last_real, last_imag = transform(along_y[:, :, :, 0], along_y[:, :, :, 1], 0, -1.0)
    rounded = jnp.stack((last_real, last_imag), 3).astype(jnp.bfloat16)
    return lax.all_to_all(rounded, "kx", split_axis=0, concat_axis=4, tiled=True)


def matrix_product(left, right):
    return jnp.dot(left, right, preferred_element_type=jnp.float32)


def complex_product(left_real, left_imag, right_real, right_imag):
    real_out = matrix_product(left_real, right_real) - matrix_product(left_imag, right_imag)
    imag_out = matrix_product(left_real, right_imag) + matrix_product(left_imag, right_real)
    return (real_out, imag_out)


def collide(momentum_self, history_local):
    adv_real = history_local[0, 0].T
    adv_imag = -history_local[0, 1].T
    ret_real, ret_imag = complex_product(
        momentum_self[0, 0], momentum_self[0, 1], history_local[0, 0], history_local[0, 1]
    )
    first_real, first_imag = complex_product(
        momentum_self[0, 0], momentum_self[0, 1], history_local[1, 0], history_local[1, 1]
    )
    second_real, second_imag = complex_product(
        momentum_self[1, 0], momentum_self[1, 1], adv_real, adv_imag
    )
    retarded = jnp.stack((ret_real, ret_imag), 0)
    lesser = jnp.stack((first_real + second_real, first_imag + second_imag), 0)
    return jnp.stack((retarded, lesser), 0)


def on_device(block, history):
    history_local = history[0, 0]
    current = block
    collision = jnp.zeros(block.shape[2:], jnp.float32)
    for iteration in range(ITERS):
        site_real, site_imag = to_sites(current)
        self_real, self_imag = self_energy(site_real, site_imag)
        momentum_self = to_momenta(self_real, self_imag)
        collision = collide(momentum_self[0, 0], history_local)
        if iteration + 1 < ITERS:
            current = (block.astype(jnp.float32) + coupling * collision[None, None]).astype(
                jnp.bfloat16
            )
    return collision[None, None]


def solution(mesh):
    in_specs = (P("kx", "ky", None, None, None, None), P("kx", "ky", None, None, None, None))
    out_specs = P("kx", "ky", None, None, None, None)
    return jax.shard_map(
        on_device, mesh=mesh, in_specs=in_specs, out_specs=out_specs, check_vma=False
    )
```

profile of v0, /device:TPU:1, one launch (start us, length us, event | category | flops | bytes accessed | tf_op | source)
XLA Modules:
  0.0 189.3 jit_solution(2225646888184967271)
XLA Ops:
  0.0 1.7 copy.90
  1.7 17.7 %all-to-all-start = ((bf16[1,1,2,2,128,128]{5,3,2,1,0,4:T(2,128)(2,1)}), bf16[1,1,2,2,128,128]{5,3,2,1,0,4:T(2,128)(2,1)S(1)}, u32[]{:S(2)}, u32[]{:S(2)}) async-start(bf16[1,1,2,2,128,128]{5,3,2,1,0,4:T(2,128)(2,1)} %copy.90), calls=%async_computation | async-start | bytes 262144 | tf_op jit(solution)/shard_map/all_to_all | solution.py:71
  19.5 10.5 %all-to-all-done = bf16[1,1,2,2,128,128]{5,3,2,1,0,4:T(2,128)(2,1)S(1)} async-done(((bf16[1,1,2,2,128,128]{5,3,2,1,0,4:T(2,128)(2,1)}), bf16[1,1,2,2,128,128]{5,3,2,1,0,4:T(2,128)(2,1)S(1)}, u32[]{:S(2)}, u32[]{:S(2)}) %all-to-all-start) | async-done | bytes 131104 | tf_op jit(solution)/shard_map/all_to_all | solution.py:71
  30.5 0.4 copy.93
  30.9 1.2 reshape.466
  32.1 12.4 %all-to-all-start.1 = ((bf16[32,2,1024]{2,1,0:T(2,128)(2,1)}), bf16[32,2,1024]{2,1,0:T(2,128)(2,1)S(1)}, u32[]{:S(2)}, u32[]{:S(2)}) async-start(bf16[32,2,1024]{2,1,0:T(2,128)(2,1)} %reshape.466), calls=%async_computation.1 | async-start | bytes 262144 | tf_op jit(solution)/shard_map/all_to_all | solution.py:76
  44.5 14.3 %all-to-all-done.1 = bf16[32,2,1024]{2,1,0:T(2,128)(2,1)S(1)} async-done(((bf16[32,2,1024]{2,1,0:T(2,128)(2,1)}), bf16[32,2,1024]{2,1,0:T(2,128)(2,1)S(1)}, u32[]{:S(2)}, u32[]{:S(2)}) %all-to-all-start.1) | async-done | bytes 131104 | tf_op jit(solution)/shard_map/all_to_all | solution.py:76
  59.6 0.5 convolution_bitcast_fusion.1
  64.2 0.9 copy.104
  65.0 0.5 reshape.468
  65.6 18.0 %all_to_all.84 = bf16[32,2,1024]{2,1,0:T(2,128)(2,1)S(1)} all-to-all(bf16[32,2,1024]{2,1,0:T(2,128)(2,1)S(1)} %reshape.468), channel_id=1, replica_groups=mesh['kx'=32,'ky'=32] {'ky'}, dimensions={0} | all-to-all | bytes 262144 | tf_op jit(solution)/shard_map/all_to_all | solution.py:88
  85.3 18.8 %all_to_all.85 = bf16[32,1,2,2,4,128]{5,4,2,3,1,0:T(4,128)(2,1)S(1)} all-to-all(bf16[32,1,2,2,4,128]{5,4,2,3,1,0:T(4,128)(2,1)S(1)} %copy.108), channel_id=1, replica_groups=mesh['kx'=32,'ky'=32] {'kx'}, dimensions={0} | all-to-all | bytes 262144 | tf_op jit(solution)/shard_map/all_to_all | solution.py:93
  104.2 0.9 copy-done
  106.8 0.9 copy-done.1
  107.9 14.9 %all_to_all.86 = bf16[1,1,2,2,128,128]{5,3,2,1,0,4:T(2,128)(2,1)S(1)} all-to-all(bf16[1,1,2,2,128,128]{5,3,2,1,0,4:T(2,128)(2,1)S(1)} %copy.110), channel_id=1, replica_groups=mesh['kx'=32,'ky'=32] {'kx'}, dimensions={4} | all-to-all | bytes 262144 | tf_op jit(solution)/shard_map/all_to_all | solution.py:71
  123.2 0.4 copy.113
  123.7 0.5 reshape.470
  124.2 17.4 %all_to_all.87 = bf16[32,2,1024]{2,1,0:T(2,128)(2,1)S(1)} all-to-all(bf16[32,2,1024]{2,1,0:T(2,128)(2,1)S(1)} %reshape.470), channel_id=1, replica_groups=mesh['kx'=32,'ky'=32] {'ky'}, dimensions={0} | all-to-all | bytes 262144 | tf_op jit(solution)/shard_map/all_to_all | solution.py:76
  142.4 0.5 convolution_bitcast_fusion
  147.0 0.9 copy.124
  147.8 0.5 reshape.472
  148.4 18.7 %all_to_all.88 = bf16[32,2,1024]{2,1,0:T(2,128)(2,1)S(1)} all-to-all(bf16[32,2,1024]{2,1,0:T(2,128)(2,1)S(1)} %reshape.472), channel_id=1, replica_groups=mesh['kx'=32,'ky'=32] {'ky'}, dimensions={0} | all-to-all | bytes 262144 | tf_op jit(solution)/shard_map/all_to_all | solution.py:88
  168.8 18.0 %all_to_all.89 = bf16[32,1,2,2,4,128]{5,4,2,3,1,0:T(4,128)(2,1)S(1)} all-to-all(bf16[32,1,2,2,4,128]{5,4,2,3,1,0:T(4,128)(2,1)S(1)} %copy.128), channel_id=1, replica_groups=mesh['kx'=32,'ky'=32] {'kx'}, dimensions={0} | all-to-all | bytes 262144 | tf_op jit(solution)/shard_map/all_to_all | solution.py:93
  188.6 0.7 maximum_bitcast_fusion.16
  (127 shorter events, 17.6 us)
Async XLA Ops:
  1.7 28.3 %all-to-all-start = ((bf16[1,1,2,2,128,128]{5,3,2,1,0,4:T(2,128)(2,1)}), bf16[1,1,2,2,128,128]{5,3,2,1,0,4:T(2,128)(2,1)S(1)}, u32[]{:S(2)}, u32[]{:S(2)}) async-start(bf16[1,1,2,2,128,128]{5,3,2,1,0,4:T(2,128)(2,1)} %copy.90), calls=%async_computation | async-start | bytes 262144 | tf_op jit(solution)/shard_map/all_to_all | solution.py:71
  32.1 26.7 %all-to-all-start.1 = ((bf16[32,2,1024]{2,1,0:T(2,128)(2,1)}), bf16[32,2,1024]{2,1,0:T(2,128)(2,1)S(1)}, u32[]{:S(2)}, u32[]{:S(2)}) async-start(bf16[32,2,1024]{2,1,0:T(2,128)(2,1)} %reshape.466), calls=%async_computation.1 | async-start | bytes 262144 | tf_op jit(solution)/shard_map/all_to_all | solution.py:76
  104.1 0.9 copy-start
  106.8 0.9 copy-start.1
where the time goes:
time: 190 us; the launch traced here: 189 us
  blocking collectives  106 us (56%)
  starting transfers between devices  30 us (16%)
  waiting for transfers between devices  24.8 us (13%)
  local copies, waits for them, and re-layouts  16.7 us (9%)
  matrix products  6.34 us (3%)
  other arithmetic  4.93 us (3%)
    all_to_all x2, blocking collectives, to_momenta(): lax.all_to_all(rounded, 'kx', split_axis=0, concat_axis=4, tiled=True)  36.8 us
    all_to_all x2, blocking collectives, to_momenta(): lax.all_to_all(shortened(stacked), 'ky', split_axis=1, concat_axis=5, til...  36.7 us
    all_to_all x1, starting transfers between devices, to_sites(): lax.all_to_all(current, 'kx', split_axis=4, concat_axis=0, tiled=True)  17.7 us
    all_to_all x1, blocking collectives, to_sites(): lax.all_to_all(shortened(stacked), 'ky', split_axis=5, concat_axis=1, til...  17.4 us
    all_to_all x1, blocking collectives, to_sites(): lax.all_to_all(current, 'kx', split_axis=4, concat_axis=0, tiled=True)  14.9 us
    all_to_all x1, waiting for transfers between devices, to_sites(): lax.all_to_all(shortened(stacked), 'ky', split_axis=5, concat_axis=1, til...  14.3 us
    all_to_all x1, starting transfers between devices, to_sites(): lax.all_to_all(shortened(stacked), 'ky', split_axis=5, concat_axis=1, til...  12.4 us
    all_to_all x1, waiting for transfers between devices, to_sites(): lax.all_to_all(current, 'kx', split_axis=4, concat_axis=0, tiled=True)  10.5 us
  transfers between devices with their start and end apart: 2, of which 2 were waited for; matrix products, arithmetic and copies ran while one was open for 0% of the time, Pallas kernels for 0%

commit v1 on v0

v1 whole, which is shorter than its diff:
```python
import math

import jax
import jax.numpy as jnp
import numpy as np
from jax import lax
from jax.experimental import pallas as pl
from jax.experimental.pallas import tpu as pltpu
from jax.sharding import PartitionSpec as P

ITERS = 2
PHASES = 4
WIDE = 128

coupling = 0.5


def tables(n):
    q = WIDE // n
    spread = np.zeros((2 * WIDE, 2 * WIDE), np.float32)
    for j in range(n):
        for c in range(2):
            for i in range(q):
                spread[j * 2 * q + c * q + i, c * WIDE + i * n + j] = 1.0
    phases = np.outer(np.arange(n), np.arange(n)) % n * (2.0 * math.pi / n)
    cosine = np.cos(phases) / math.sqrt(n)
    sine = np.sin(phases) / math.sqrt(n)
    mixed = np.stack((np.stack((cosine, sine), 1), np.stack((-sine, cosine), 1)), 1)
    to_site = np.einsum("kcdx,ij->kcidxj", mixed, np.eye(q)).reshape(2 * WIDE, 2 * WIDE)
    back = (-np.arange(n)) % n
    forward = to_site.T.reshape(2, n, q, 2 * WIDE)
    mirrored = forward[:, back].reshape(2 * WIDE, 2 * WIDE)
    flip = np.einsum("xy,ij->xiyj", np.eye(n)[back], np.eye(q)).reshape(WIDE, WIDE)
    parts = (spread, spread.T, to_site, to_site.T, mirrored, flip)
    return [jnp.asarray(part, jnp.bfloat16) for part in parts]


def product(left, right, dims=((1,), (0,))):
    return lax.dot_general(left, right, (dims, ((), ())), preferred_element_type=jnp.float32)


def short(x):
    return x.astype(jnp.bfloat16)


def kernel(
    n,
    block,
    history,
    spread,
    gather,
    to_momentum,
    to_site,
    to_mirror,
    flip,
    out,
    outgoing,
    incoming,
    right_side,
    send_sem,
    recv_sem,
):
    q = WIDE // n
    half = 2 * q
    place = {"kx": lax.axis_index("kx"), "ky": lax.axis_index("ky")}
    barrier = pltpu.get_barrier_semaphore()

    @pl.loop(1, n)
    def _(step):
        for axis in ("kx", "ky"):
            peer = lax.rem(place[axis] + step, n)
            pl.semaphore_signal(
                barrier, inc=1, device_id={axis: peer}, device_id_type=pl.DeviceIdType.MESH
            )

    def post(slot, kinds):
        tiles = [part.reshape(n, half, WIDE) for part in kinds]
        outgoing[slot] = short(jnp.concatenate(tiles, 1))

    def launch(slot, axis):
        me = place[axis]

        @pl.loop(1, n)
        def _(step):
            far = n // 2 - step // 2 + lax.rem(step, 2) * (2 * (step // 2))
            peer = lax.rem(me + far, n)
            pltpu.make_async_remote_copy(
                src_ref=outgoing.at[slot, peer],
                dst_ref=incoming.at[slot, me],
                send_sem=send_sem.at[slot],
                recv_sem=recv_sem.at[slot],
                device_id={axis: peer},
                device_id_type=pl.DeviceIdType.MESH,
            ).start()

        incoming[slot, me] = outgoing[slot, me]

    def everything(slot, axis):
        return pltpu.make_async_remote_copy(
            src_ref=outgoing.at[slot, pl.ds(0, n - 1)],
            dst_ref=incoming.at[slot, pl.ds(0, n - 1)],
            send_sem=send_sem.at[slot],
            recv_sem=recv_sem.at[slot],
            device_id={axis: lax.rem(place[axis] + 1, n)},
            device_id_type=pl.DeviceIdType.MESH,
        )

    def take(slot, axis):
        everything(slot, axis).wait_recv()
        tiles = incoming[slot].astype(jnp.float32)
        return [
            short(tiles[:, kind * half : (kind + 1) * half].reshape(2 * WIDE, WIDE))
            for kind in range(2)
        ]

    def exchange(slot, axis, kinds):
        post(slot, kinds)
        launch(slot, axis)
        return take(slot, axis)

    def stacked(wide):
        return jnp.concatenate((wide[:, :WIDE], wide[:, WIDE:]), 0)

    def side_by_side(tall):
        return jnp.concatenate((tall[:WIDE], tall[WIDE:]), 1)

    for kind in range(2):
        for part in range(2):
            piece = history[kind, part]
            rows, lanes = kind * 2 * WIDE, part * WIDE
            right_side[rows : rows + WIDE, lanes : lanes + WIDE] = piece
            other = (1 - part) * WIDE
            turned = piece if part == 0 else -piece
            right_side[rows + WIDE : rows + 2 * WIDE, other : other + WIDE] = turned
    for part in range(2):
        piece = history[0, part].astype(jnp.float32).T
        adjoint = short(piece if part == 0 else -piece)
        rows, lanes = 4 * WIDE, part * WIDE
        right_side[rows : rows + WIDE, lanes : lanes + WIDE] = adjoint
        other = (1 - part) * WIDE
        turned = adjoint if part == 0 else -adjoint
        right_side[rows + WIDE : rows + 2 * WIDE, other : other + WIDE] = turned

    start = [block[kind].reshape(2 * WIDE, WIDE) for kind in range(2)]
    current = start
    for iteration in range(ITERS):
        slot = iteration * PHASES
        post(slot, [product(spread[...], current[kind]) for kind in range(2)])
        if iteration == 0:
            pl.semaphore_wait(barrier, 2 * (n - 1))
        launch(slot, "kx")
        rows_in = take(slot, "kx")
        half_way = []
        for kind in range(2):
            turned = product(rows_in[kind], to_momentum[...], ((0,), (0,)))
            half_way.append(product(spread[...], short(stacked(turned))))
        columns_in = exchange(slot + 1, "ky", half_way)
        green, mirror = [], []
        for kind in range(2):
            site = product(to_site[...], columns_in[kind])
            green.append((site[:WIDE], site[WIDE:]))
            flipped = short(product(columns_in[kind], flip[...]))
            site = product(to_mirror[...], flipped)
            mirror.append((site[:WIDE], site[WIDE:]))
        selves = []
        for kind in range(2):
            real, imag = green[kind]
            other_real, other_imag = mirror[1 - kind]
            square_real = real * real - imag * imag
            square_imag = real * imag + imag * real
            self_real = square_real * other_real + square_imag * other_imag
            self_imag = square_imag * other_real - square_real * other_imag
            selves.append(short(jnp.concatenate((self_real, self_imag), 0)))
        half_back = exchange(
            slot + 2, "ky", [product(to_momentum[...], selves[kind]) for kind in range(2)]
        )
        last = []
        for kind in range(2):
            regrouped = side_by_side(short(product(gather[...], half_back[kind])))
            last.append(product(to_momentum[...], regrouped, ((1,), (1,))))
        whole = exchange(slot + 3, "kx", last)
        sides = [
            side_by_side(short(product(gather[...], whole[kind]))) for kind in range(2)
        ]
        retarded = product(sides[0], right_side[0 : 2 * WIDE])
        lesser = product(
            jnp.concatenate(sides, 1), right_side[2 * WIDE : 6 * WIDE]
        )
        collision = [stacked(retarded), stacked(lesser)]
        if iteration + 1 < ITERS:
            current = [
                short(start[kind].astype(jnp.float32) + coupling * collision[kind])
                for kind in range(2)
            ]
    for kind in range(2):
        out[kind] = collision[kind].reshape(2, WIDE, WIDE)
    for slot in range(ITERS * PHASES):
        axis = "kx" if slot % PHASES in (0, 3) else "ky"
        everything(slot, axis).wait_send()


def solution(mesh):
    n = mesh.shape["kx"]
    slots = ITERS * PHASES
    spec = P("kx", "ky", None, None, None, None)

    def on_device(block, history):
        result = pl.pallas_call(
            lambda *refs: kernel(n, *refs),
            out_shape=jax.ShapeDtypeStruct((2, 2, WIDE, WIDE), jnp.float32),
            in_specs=[pl.BlockSpec(memory_space=pltpu.VMEM)] * 8,
            out_specs=pl.BlockSpec(memory_space=pltpu.VMEM),
            scratch_shapes=[
                pltpu.VMEM((slots, n, 4 * WIDE // n, WIDE), jnp.bfloat16),
                pltpu.VMEM((slots, n, 4 * WIDE // n, WIDE), jnp.bfloat16),
                pltpu.VMEM((6 * WIDE, 2 * WIDE), jnp.bfloat16),
                pltpu.SemaphoreType.DMA((slots,)),
                pltpu.SemaphoreType.DMA((slots,)),
            ],
            compiler_params=pltpu.CompilerParams(collective_id=0, has_side_effects=True),
        )(block[0, 0], history[0, 0], *tables(n))
        return result[None, None]

    return jax.shard_map(
        on_device, mesh=mesh, in_specs=(spec, spec), out_specs=spec, check_vma=False
    )
```

time: 190 us -> 100 us (0.53)
  blocking collectives: 106 us -> 0 us
  Pallas kernels: 0 us -> 98.5 us
  starting transfers between devices: 30 us -> 0 us
  waiting for transfers between devices: 24.8 us -> 0 us
  local copies, waits for them, and re-layouts: 16.7 us -> 1.67 us
  matrix products: 6.34 us -> 0 us
  other arithmetic: 4.93 us -> 0 us
    all_to_all x6 -> x0, blocking collectives: 106 us -> none  [the longest x2 36.8 us: to_momenta(): lax.all_to_all(rounded, 'kx', split_axis=0, concat_axis=4, tiled=True)]
    pallas_call x0 -> x1, Pallas kernels: none -> 98.5 us  [on_device(): pl.pallas_call(lambda *refs: kernel(n, *refs), out_shape=jax.ShapeDtypeSt...]
    all_to_all x2 -> x0, starting transfers between devices: 30 us -> none  [the longest x1 17.7 us: to_sites(): lax.all_to_all(current, 'kx', split_axis=4, concat_axis=0, tiled=True)]
    all_to_all x2 -> x0, waiting for transfers between devices: 24.8 us -> none  [the longest x1 14.3 us: to_sites(): lax.all_to_all(shortened(stacked), 'ky', split_axis=5, concat_axis=1, til...]
    dot_general x32 -> x0, matrix products: 6.34 us -> none  [the longest x24 3.39 us: matrix_product(): return jnp.dot(left, right, preferred_element_type=jnp.float32)]
    unnamed x17 -> x1, local copies, waits for them, and re-layouts: 7.92 us -> 1.67 us
    slice x22 -> x0, local copies, waits for them, and re-layouts: 3.95 us -> none  [the longest x20 3.76 us: mirror(): return jnp.roll(jnp.flip(field, (0, 1)), (1, 1), (0, 1))]
    another operation x12 -> x0, local copies, waits for them, and re-layouts: 3.02 us -> none  [the longest x4 1.98 us: to_momenta(): stacked = jnp.stack((first_real, first_imag), 3)]
  transfers between devices with their start and end apart: 2 -> 0, of which waited for: 2 -> 0; matrix products, arithmetic and copies ran while one was open for 0% -> 0% of each run, Pallas kernels for 0% -> 0%
where the time goes in v1:
time: 100 us
  Pallas kernels  98.5 us (98%)
  local copies, waits for them, and re-layouts  1.67 us (2%)
    pallas_call x1, Pallas kernels, on_device(): pl.pallas_call(lambda *refs: kernel(n, *refs), out_shape=jax.ShapeDtypeSt...  98.5 us

profile of v1, /device:TPU:1, one launch (start us, length us, event | category | flops | bytes accessed | tf_op | source)
XLA Modules:
  0.0 100.2 jit_solution(14604913790536756674)
XLA Ops:
  0.0 98.5 %shard_map.82 = f32[2,2,128,128]{3,2,1,0:T(8,128)} custom-call(bf16[2,2,128,128]{3,2,1,0:T(8,128)(2,1)} %bitcast.4, bf16[2,2,128,128]{3,2,1,0:T(8,128)(2,1)} %bitcast.5, bf16[256,256]{1,0:T(8,128)(2,1)} %constant.12.clone.refs_2_, bf16[256,256]{1,0:T(8,128)(2,1)} %constant.13.clone.refs_3_, bf16[256,256]{1,0:T(8,128)(2,1)} %constant.14.clone.refs_4_, ...), custom_call_target="tpu_custom_call" | custom-call | tf_op jit(solution)/shard_map/pallas_call | solution.py:208
  98.5 1.7 %copy.10 = f32[1,1,2,2,128,128]{5,4,3,2,1,0:T(8,128)} copy(f32[1,1,2,2,128,128]{5,4,3,2,1,0:T(8,128)} %bitcast.3) | data formatting | bytes 524288

commit v2 on v1

v2 whole, which is shorter than its diff:
```python
import math

import jax
import jax.numpy as jnp
import numpy as np
from jax import lax
from jax.experimental import pallas as pl
from jax.experimental.pallas import tpu as pltpu
from jax.sharding import PartitionSpec as P

ITERS = 2
PHASES = 4
CHUNKS = 2
WIDE = 128
STRETCH = 1.62175

coupling = 0.5


def tables(n):
    q = WIDE // n
    part = q // CHUNKS
    unit = np.eye(2 * WIDE, dtype=np.float32)
    spread = unit.reshape(2, q, n, -1).transpose(2, 0, 1, 3).reshape(2 * WIDE, -1)
    first = unit.reshape(4, part, n, -1).transpose(2, 0, 1, 3).reshape(2 * WIDE, -1)
    phases = np.outer(np.arange(n), np.arange(n)) % n * (2.0 * math.pi / n)
    cosine = np.cos(phases)
    sine = np.sin(phases)
    mixed = np.stack((np.stack((cosine, sine), 1), np.stack((-sine, cosine), 1)), 1)
    along_y = np.einsum("kcdx,ij->kcidxj", mixed, np.eye(q)).reshape(2 * WIDE, 2 * WIDE)
    along_x = np.einsum(
        "kcdx,ij,st->kscidtxj", mixed, np.eye(part), np.eye(2)
    ).reshape(2 * WIDE, 2 * WIDE)
    back = (-np.arange(n)) % n
    mirrored = along_y.T.reshape(2, n, q, 2 * WIDE)[:, back].reshape(2 * WIDE, 2 * WIDE)
    flip = np.einsum(
        "st,xy,ij->sxityj", np.eye(2)[::-1], np.eye(n)[back], np.eye(part)
    ).reshape(WIDE, WIDE)

    def scaled(table):
        return jnp.asarray(table * STRETCH, jnp.bfloat16)

    held = (cosine * STRETCH).astype(jnp.bfloat16).astype(np.float64)
    factor = float((held * cosine).sum() / (held * held).sum() / math.sqrt(n))
    exact = [jnp.asarray(table, jnp.bfloat16) for table in (spread, spread.T, first, first.T, flip)]
    return factor, exact + [scaled(t) for t in (along_x, along_y, along_y.T, mirrored)]


def product(left, right, dims=((1,), (0,))):
    return lax.dot_general(left, right, (dims, ((), ())), preferred_element_type=jnp.float32)


def short(x):
    return x.astype(jnp.bfloat16)


def kernel(
    n,
    factor,
    block,
    history,
    spread,
    gather,
    first_spread,
    first_gather,
    flip,
    along_x,
    along_y,
    to_site,
    to_mirror,
    out,
    outgoing,
    incoming,
    right_side,
    send_sem,
    recv_sem,
):
    rows = WIDE // CHUNKS
    place = {"kx": lax.axis_index("kx"), "ky": lax.axis_index("ky")}
    barrier = pltpu.get_barrier_semaphore()

    @pl.loop(1, n)
    def _(step):
        for axis in ("kx", "ky"):
            peer = lax.rem(place[axis] + step, n)
            pl.semaphore_signal(
                barrier, inc=1, device_id={axis: peer}, device_id_type=pl.DeviceIdType.MESH
            )

    def axis_of(slot):
        return "kx" if slot // CHUNKS % PHASES in (0, 3) else "ky"

    def post(slot, tall):
        outgoing[slot] = short(tall.reshape(outgoing.shape[1:]))

    def launch(slot):
        axis = axis_of(slot)
        me = place[axis]

        @pl.loop(1, n)
        def _(step):
            far = n // 2 - step // 2 + lax.rem(step, 2) * (2 * (step // 2))
            peer = lax.rem(me + far, n)
            pltpu.make_async_remote_copy(
                src_ref=outgoing.at[slot, peer],
                dst_ref=incoming.at[slot, me],
                send_sem=send_sem.at[slot],
                recv_sem=recv_sem.at[slot],
                device_id={axis: peer},
                device_id_type=pl.DeviceIdType.MESH,
            ).start()

        incoming[slot, me] = outgoing[slot, me]

    def everything(slot):
        axis = axis_of(slot)
        return pltpu.make_async_remote_copy(
            src_ref=outgoing.at[slot, pl.ds(0, n - 1)],
            dst_ref=incoming.at[slot, pl.ds(0, n - 1)],
            send_sem=send_sem.at[slot],
            recv_sem=recv_sem.at[slot],
            device_id={axis: lax.rem(place[axis] + 1, n)},
            device_id_type=pl.DeviceIdType.MESH,
        )

    def take(slot):
        everything(slot).wait_recv()
        return short(incoming[slot].astype(jnp.float32).reshape(2 * WIDE, WIDE))

    def stacked(wide):
        return jnp.concatenate((wide[:, :WIDE], wide[:, WIDE:]), 0)

    def side_by_side(tall):
        return jnp.concatenate((tall[:WIDE], tall[WIDE:]), 1)

    def rows_of(chunk):
        return [
            block[kind, part, chunk * rows : (chunk + 1) * rows]
            for kind in range(2)
            for part in range(2)
        ]

    def leave(chunk, received):
        turned = product(received, along_x[...], ((0,), (0,))) * factor
        return product(spread[...], short(stacked(turned)))

    def at_sites(chunk, received):
        site = product(to_site[...], received) * factor
        flipped = short(product(received, flip[...]))
        other = product(to_mirror[...], flipped) * factor
        real, imag = site[:WIDE], site[WIDE:]
        other_real, other_imag = other[:WIDE], other[WIDE:]
        square_real = real * real - imag * imag
        square_imag = real * imag + imag * real
        self_real = square_real * other_real + square_imag * other_imag
        self_imag = square_imag * other_real - square_real * other_imag
        selves = short(jnp.concatenate((self_real, self_imag), 0))
        return product(along_y[...], selves) * factor

    def come_back(chunk, received):
        regrouped = side_by_side(short(product(gather[...], received)))
        return product(along_x[...], regrouped, ((1,), (1,))) * factor

    def collide(chunk, received):
        whole = short(product(first_gather[...], received))
        sides = [whole[index * rows : (index + 1) * rows] for index in range(4)]
        retarded = product(jnp.concatenate(sides[:2], 1), right_side[0 : 2 * WIDE])
        lesser = product(jnp.concatenate(sides, 1), right_side[2 * WIDE : 6 * WIDE])
        return [
            result[:, part * WIDE : (part + 1) * WIDE]
            for result in (retarded, lesser)
            for part in range(2)
        ]

    def renew(chunk, received):
        collision = collide(chunk, received)
        current = [
            short(old.astype(jnp.float32) + coupling * new)
            for old, new in zip(rows_of(chunk), collision)
        ]
        return product(first_spread[...], jnp.concatenate(current, 0))

    for chunk in range(CHUNKS):
        post(chunk, product(first_spread[...], jnp.concatenate(rows_of(chunk), 0)))
    pl.semaphore_wait(barrier, 2 * (n - 1))
    for chunk in range(CHUNKS):
        launch(chunk)

    for kind in range(2):
        for part in range(2):
            piece = history[kind, part]
            top, lanes = kind * 2 * WIDE, part * WIDE
            right_side[top : top + WIDE, lanes : lanes + WIDE] = piece
            other = (1 - part) * WIDE
            turned = piece if part == 0 else -piece
            right_side[top + WIDE : top + 2 * WIDE, other : other + WIDE] = turned
    for part in range(2):
        piece = history[0, part].astype(jnp.float32).T
        adjoint = short(piece if part == 0 else -piece)
        top, lanes = 4 * WIDE, part * WIDE
        right_side[top : top + WIDE, lanes : lanes + WIDE] = adjoint
        other = (1 - part) * WIDE
        turned = adjoint if part == 0 else -adjoint
        right_side[top + WIDE : top + 2 * WIDE, other : other + WIDE] = turned

    steps = ITERS * (leave, at_sites, come_back, renew)
    for phase in range(ITERS * PHASES - 1):
        for chunk in range(CHUNKS):
            slot = phase * CHUNKS + chunk
            post(slot + CHUNKS, steps[phase](chunk, take(slot)))
            launch(slot + CHUNKS)
    for chunk in range(CHUNKS):
        collision = collide(chunk, take((ITERS * PHASES - 1) * CHUNKS + chunk))
        for index in range(4):
            out[index // 2, index % 2, chunk * rows : (chunk + 1) * rows] = collision[index]
    for slot in range(ITERS * PHASES * CHUNKS):
        everything(slot).wait_send()


def solution(mesh):
    n = mesh.shape["kx"]
    slots = ITERS * PHASES * CHUNKS
    tiles = (slots, n, 2 * WIDE // n, WIDE)
    spec = P("kx", "ky", None, None, None, None)

    def on_device(block, history):
        factor, held = tables(n)
        result = pl.pallas_call(
            lambda *refs: kernel(n, factor, *refs),
            out_shape=jax.ShapeDtypeStruct((2, 2, WIDE, WIDE), jnp.float32),
            in_specs=[pl.BlockSpec(memory_space=pltpu.VMEM)] * (2 + len(held)),
            out_specs=pl.BlockSpec(memory_space=pltpu.VMEM),
            scratch_shapes=[
                pltpu.VMEM(tiles, jnp.bfloat16),
                pltpu.VMEM(tiles, jnp.bfloat16),
                pltpu.VMEM((6 * WIDE, 2 * WIDE), jnp.bfloat16),
                pltpu.SemaphoreType.DMA((slots,)),
                pltpu.SemaphoreType.DMA((slots,)),
            ],
            compiler_params=pltpu.CompilerParams(collective_id=0, has_side_effects=True),
        )(block[0, 0], history[0, 0], *held)
        return result[None, None]

    return jax.shard_map(
        on_device, mesh=mesh, in_specs=(spec, spec), out_specs=spec, check_vma=False
    )
```

time: 100 us -> 94.7 us (0.947)
  Pallas kernels: 98.5 us -> 92.8 us
    pallas_call x1, Pallas kernels: 98.5 us -> 92.8 us  [on_device(): pl.pallas_call(lambda *refs: kernel(n, factor, *refs), out_shape=jax.Shap...]
where the time goes in v2:
time: 94.7 us; the launch traced here: 94.5 us
  Pallas kernels  92.8 us (98%)
  local copies, waits for them, and re-layouts  1.67 us (2%)
    pallas_call x1, Pallas kernels, on_device(): pl.pallas_call(lambda *refs: kernel(n, factor, *refs), out_shape=jax.Shap...  92.8 us

profile of v2, /device:TPU:1, one launch (start us, length us, event | category | flops | bytes accessed | tf_op | source)
XLA Modules:
  0.0 94.5 jit_solution(15043665621863673889)
XLA Ops:
  0.0 92.8 %shard_map.109 = f32[2,2,128,128]{3,2,1,0:T(8,128)} custom-call(bf16[2,2,128,128]{3,2,1,0:T(8,128)(2,1)} %bitcast.4, bf16[2,2,128,128]{3,2,1,0:T(8,128)(2,1)} %bitcast.5, bf16[256,256]{1,0:T(8,128)(2,1)} %constant.14.clone.refs_2_.refs_4_, bf16[256,256]{1,0:T(8,128)(2,1)} %constant.15.clone.refs_3_.refs_5_, bf16[256,256]{1,0:T(8,128)(2,1)} %constant.14.clone.refs_2_.refs_4_, ...), custom_call_target="tpu_custom_call" | custom-call | tf_op jit(solution)/shard_map/pallas_call | solution.py:228
  92.9 1.7 %copy.13 = f32[1,1,2,2,128,128]{5,4,3,2,1,0:T(8,128)} copy(f32[1,1,2,2,128,128]{5,4,3,2,1,0:T(8,128)} %bitcast.3) | data formatting | bytes 524288

commit v3 on v2

--- a/solution.py
+++ b/solution.py
@@ -42,8 +42,13 @@
 
     held = (cosine * STRETCH).astype(jnp.bfloat16).astype(np.float64)
     factor = float((held * cosine).sum() / (held * held).sum() / math.sqrt(n))
-    exact = [jnp.asarray(table, jnp.bfloat16) for table in (spread, spread.T, first, first.T, flip)]
-    return factor, exact + [scaled(t) for t in (along_x, along_y, along_y.T, mirrored)]
+    def plain(table):
+        return jnp.asarray(table, jnp.bfloat16)
+
+    before = [plain(first)]
+    after = [scaled(along_x), plain(spread), scaled(along_y.T), plain(flip)]
+    after += [scaled(mirrored), scaled(along_y), plain(spread.T), plain(first.T)]
+    return factor, before, after
 
 
 def product(left, right, dims=((1,), (0,))):
@@ -57,24 +62,13 @@
 def kernel(
     n,
     factor,
-    block,
-    history,
-    spread,
-    gather,
-    first_spread,
-    first_gather,
-    flip,
-    along_x,
-    along_y,
-    to_site,
-    to_mirror,
-    out,
-    outgoing,
-    incoming,
-    right_side,
-    send_sem,
-    recv_sem,
+    count,
+    *refs,
 ):
+    sources, out, held = refs[:count], refs[count], refs[count + 1 : 2 * count + 1]
+    outgoing, incoming, right_side, send_sem, recv_sem, load_sem = refs[2 * count + 1 :]
+    block, first_spread, history, along_x, spread, to_site, flip = held[:7]
+    to_mirror, along_y, gather, first_gather = held[7:]
     rows = WIDE // CHUNKS
     place = {"kx": lax.axis_index("kx"), "ky": lax.axis_index("ky")}
     barrier = pltpu.get_barrier_semaphore()
@@ -87,8 +81,16 @@
                 barrier, inc=1, device_id={axis: peer}, device_id_type=pl.DeviceIdType.MESH
             )
 
+    loads = [
+        pltpu.make_async_copy(source, target, load_sem.at[index])
+        for index, (source, target) in enumerate(zip(sources, held))
+    ]
+    for load in loads:
+        load.start()
+
     def axis_of(slot):
-        return "kx" if slot // CHUNKS % PHASES in (0, 3) else "ky"
+        outer = slot // CHUNKS % PHASES in (0, 3)
+        return "kx" if outer == (slot % CHUNKS == 0) else "ky"
 
     def post(slot, tall):
         outgoing[slot] = short(tall.reshape(outgoing.shape[1:]))
@@ -97,10 +99,8 @@
         axis = axis_of(slot)
         me = place[axis]
 
-        @pl.loop(1, n)
-        def _(step):
-            far = n // 2 - step // 2 + lax.rem(step, 2) * (2 * (step // 2))
-            peer = lax.rem(me + far, n)
+        def send(away):
+            peer = lax.rem(me + away, n)
             pltpu.make_async_remote_copy(
                 src_ref=outgoing.at[slot, peer],
                 dst_ref=incoming.at[slot, me],
@@ -110,6 +110,18 @@
                 device_id_type=pl.DeviceIdType.MESH,
             ).start()
 
+        send(n // 4)
+        send(n - n // 4)
+
+        @pl.loop(1, n // 4)
+        def _(step):
+            ring = n // 4 - step
+            send(n // 2 - ring)
+            send(n // 2 + ring)
+            send(ring)
+            send(n - ring)
+
+        send(n // 2)
         incoming[slot, me] = outgoing[slot, me]
 
     def everything(slot):
@@ -180,11 +192,15 @@
         ]
         return product(first_spread[...], jnp.concatenate(current, 0))
 
+    for load in loads[:2]:
+        load.wait()
     for chunk in range(CHUNKS):
         post(chunk, product(first_spread[...], jnp.concatenate(rows_of(chunk), 0)))
     pl.semaphore_wait(barrier, 2 * (n - 1))
     for chunk in range(CHUNKS):
         launch(chunk)
+    for load in loads[2:]:
+        load.wait()
 
     for kind in range(2):
         for part in range(2):
@@ -224,21 +240,24 @@
     spec = P("kx", "ky", None, None, None, None)
 
     def on_device(block, history):
-        factor, held = tables(n)
+        factor, before, after = tables(n)
+        operands = [block[0, 0], *before, history[0, 0], *after]
         result = pl.pallas_call(
-            lambda *refs: kernel(n, factor, *refs),
+            lambda *refs: kernel(n, factor, len(operands), *refs),
             out_shape=jax.ShapeDtypeStruct((2, 2, WIDE, WIDE), jnp.float32),
-            in_specs=[pl.BlockSpec(memory_space=pltpu.VMEM)] * (2 + len(held)),
+            in_specs=[pl.BlockSpec(memory_space=pl.ANY)] * len(operands),
             out_specs=pl.BlockSpec(memory_space=pltpu.VMEM),
-            scratch_shapes=[
+            scratch_shapes=[pltpu.VMEM(part.shape, part.dtype) for part in operands]
+            + [
                 pltpu.VMEM(tiles, jnp.bfloat16),
                 pltpu.VMEM(tiles, jnp.bfloat16),
                 pltpu.VMEM((6 * WIDE, 2 * WIDE), jnp.bfloat16),
                 pltpu.SemaphoreType.DMA((slots,)),
                 pltpu.SemaphoreType.DMA((slots,)),
+                pltpu.SemaphoreType.DMA((len(operands),)),
             ],
             compiler_params=pltpu.CompilerParams(collective_id=0, has_side_effects=True),
-        )(block[0, 0], history[0, 0], *held)
+        )(*operands)
         return result[None, None]
 
     return jax.shard_map(

time: 94.7 us -> 86.9 us (0.918)
  Pallas kernels: 92.8 us -> 84.9 us
    pallas_call x1, Pallas kernels: 92.8 us -> 84.9 us  [on_device(): pl.pallas_call(lambda *refs: kernel(n, factor, len(operands), *refs), out...]
where the time goes in v3:
time: 86.9 us; the launch traced here: 86.6 us
  Pallas kernels  84.9 us (98%)
  local copies, waits for them, and re-layouts  1.67 us (2%)
    pallas_call x1, Pallas kernels, on_device(): pl.pallas_call(lambda *refs: kernel(n, factor, len(operands), *refs), out...  84.9 us

profile of v3, /device:TPU:1, one launch (start us, length us, event | category | flops | bytes accessed | tf_op | source)
XLA Modules:
  0.0 86.6 jit_solution(8322726824037179154)
XLA Ops:
  0.0 84.9 %shard_map.109 = f32[2,2,128,128]{3,2,1,0:T(8,128)} custom-call(bf16[2,2,128,128]{3,2,1,0:T(8,128)(2,1)} %bitcast.4, bf16[256,256]{1,0:T(8,128)(2,1)} %constant.14.clone.refs_1_.refs_4_, bf16[2,2,128,128]{3,2,1,0:T(8,128)(2,1)} %bitcast.5, bf16[256,256]{1,0:T(8,128)(2,1)} %constant.15.clone.refs_3_, bf16[256,256]{1,0:T(8,128)(2,1)} %constant.14.clone.refs_1_.refs_4_, ...), custom_call_target="tpu_custom_call" | custom-call | tf_op jit(solution)/shard_map/pallas_call | solution.py:245
  85.0 1.7 %copy.13 = f32[1,1,2,2,128,128]{5,4,3,2,1,0:T(8,128)} copy(f32[1,1,2,2,128,128]{5,4,3,2,1,0:T(8,128)} %bitcast.3) | data formatting | bytes 524288
